TPU v7x, 128 devices: a whole 4x4x4 slice. The times are simulated.
128 devices in a mesh: sec: 2 (over z_lo), row: 8 (over x, z_hi), col: 8 (over y, core).
Axes of the slice: x: 4, y: 4, z: 4 (z_hi: 2, z_lo: 2; z = z_hi * 2 + z_lo), core: 2. Of those that a mesh axis runs over, the one named last changes fastest.
Arguments:
- held_inverse: bfloat16 [12288, 12288], P('row', ('sec', 'col')), as said below
- factor_panels: bfloat16 [2, 12288, 1024], P(None, ('sec', 'col'), 'row'), may hold values from -0.125 to 0.125
- block_inverses: bfloat16 [2, 1024, 1024], P(None, 'row'), as said below
- covariance: float32 [12288, 12288], P('row', ('sec', 'col')), may hold values from -0.9 to 0.9
Outputs:
- updated: float32 [12288, 12288], P('row', ('sec', 'col'))
Inputs may be any that keep to these rules, and one draw needn't show every extreme that they name: held_inverse is lower triangular with a positive diagonal. Each block of block_inverses is lower triangular with a positive diagonal.
All inputs are finite; a program needn't handle non-finite values.
Results may differ from a plain program's by a relative error of at most 0.0038.
Values may be sent and summed in bfloat16 or wider, within the bound.
A program may use at most 128 MiB of HBM per device.

v0:
```python
import jax
import jax.numpy as jnp
from jax import lax
from jax.sharding import Mesh
from jax.sharding import PartitionSpec as P

PANELS = 2
ROW = ("row_0", "row_1")


def scatter_axes(x, axes, dim):
    for axis in axes:
        x = lax.psum_scatter(x, axis, scatter_dimension=dim, tiled=True)
    return x


def from_root(x, axis, root):
    mine = lax.axis_index(axis) == root
    return lax.psum(jnp.where(mine, x, jnp.zeros_like(x)), axis)


def body(held_inverse, factor_panels, block_inverses, covariance):
    total = covariance
    tile_cols = held_inverse.shape[1]
    groups = lax.axis_size(("sec", "col"))
    ratio = groups // lax.axis_size(ROW)
    column_index = lax.axis_index(("sec", "col"))
    root_row = column_index // ratio
    offset = column_index % ratio * tile_cols
    for panel in range(PANELS):
        partial_value = jnp.dot(
            factor_panels[panel], block_inverses[panel], preferred_element_type=jnp.float32
        )
        scaled = scatter_axes(partial_value, ROW, 1).astype(jnp.bfloat16)
        terms = jnp.dot(
            held_inverse,
            lax.all_gather(scaled, ROW, axis=1, tiled=True),
            preferred_element_type=jnp.float32,
        )
        summed = lax.psum(terms, ("sec", "col"))
        inverse = (-summed).astype(jnp.bfloat16)
        own_block = lax.dynamic_slice_in_dim(inverse, offset, tile_cols, 0)
        column_block = from_root(own_block, ROW, root_row)
        total = total + lax.dot_general(
            inverse, column_block, (((1,), (1,)), ((), ())), preferred_element_type=jnp.float32
        )
    return total


def solution(mesh):
    split = Mesh(
        mesh.devices.reshape(mesh.shape["sec"], 4, 2, mesh.shape["col"]),
        ("sec", "row_0", "row_1", "col"),
    )
    in_specs = (
        P(ROW, ("sec", "col")),
        P(None, ("sec", "col"), ROW),
        P(None, ROW, None),
        P(ROW, ("sec", "col")),
    )
    out_specs = P(ROW, ("sec", "col"))
    return jax.shard_map(body, mesh=split, in_specs=in_specs, out_specs=out_specs, check_vma=False)
```

profile of v0, /device:TPU:5, one launch (start us, length us, event | category | flops | bytes accessed | tf_op | source)
XLA Modules:
  0.0 585.9 jit_solution(17937898365134801965)
XLA Ops:
  6.5 0.0 copy-start
  6.5 0.0 copy-start.4
  6.5 0.0 copy-start.5
  6.5 0.0 reduce-scatter.5.cloned.1.call-start
  6.5 3.4 fusion.2
  10.0 0.0 reduce-scatter.5.cloned.1.call-update
  10.0 0.0 reduce-scatter.9.cloned.1.call-start
  10.0 0.0 copy-done.4
  10.0 0.0 copy-done.5
  10.1 2.2 fusion
  12.3 0.0 reduce-scatter.9.cloned.1.call-update
  12.3 0.0 reduce-scatter.7.cloned.1.call-start
  12.3 36.8 %reduce-scatter.5.cloned.1.call-done = f32[768,256]{1,0:T(8,128)} async-done(((f32[768,1024]{1,0:T(8,128)}), f32[768,256]{1,0:T(8,128)}) %reduce-scatter.5.cloned.1.call-update) | async-done | bytes 786448 | tf_op jit(solution)/shard_map/reduce_scatter | solution.py:13
  49.2 0.0 reduce-scatter.7.cloned.1.call-update
  49.2 0.0 reduce-scatter.11.cloned.1.call-start
  49.2 40.3 %reduce-scatter.9.cloned.1.call-done = f32[768,256]{1,0:T(8,128)} async-done(((f32[768,1024]{1,0:T(8,128)}), f32[768,256]{1,0:T(8,128)}) %reduce-scatter.9.cloned.1.call-update) | async-done | bytes 786448 | tf_op jit(solution)/shard_map/reduce_scatter | solution.py:13
  89.6 0.0 reduce-scatter.11.cloned.1.call-update
  89.6 0.0 all-gather.3.cloned.1.call-start
  89.6 25.2 %reduce-scatter.7.cloned.1.call-done = f32[768,128]{1,0:T(8,128)} async-done(((f32[768,256]{1,0:T(8,128)}), f32[768,128]{1,0:T(8,128)}) %reduce-scatter.7.cloned.1.call-update) | async-done | bytes 393232 | tf_op jit(solution)/shard_map/reduce_scatter | solution.py:13
  114.8 1.7 convert_element_type.12
  116.5 0.0 all-gather.3.cloned.1.call-update
  116.6 0.0 all-gather.5.cloned.1.call-start
  116.6 21.3 %reduce-scatter.11.cloned.1.call-done = f32[768,128]{1,0:T(8,128)} async-done(((f32[768,256]{1,0:T(8,128)}), f32[768,128]{1,0:T(8,128)}) %reduce-scatter.11.cloned.1.call-update) | async-done | bytes 393232 | tf_op jit(solution)/shard_map/reduce_scatter | solution.py:13
  138.0 1.7 convert_element_type.14
  139.7 0.0 all-gather.5.cloned.1.call-update
  139.7 0.0 all-reduce.5.cloned.1.call-start
  139.7 49.3 %all-gather.3.cloned.1.call-done = bf16[768,1024]{1,0:T(8,128)(2,1)} async-done(((bf16[768,128]{1,0:T(8,128)(2,1)}), bf16[768,1024]{1,0:T(8,128)(2,1)}) %all-gather.3.cloned.1.call-update) | async-done | bytes 1572880 | tf_op jit(solution)/shard_map/all_gather | solution.py:37
  189.0 0.0 copy-done
  189.0 6.1 %convolution_bitcast_fusion.1 = f32[1536,1024]{0,1:T(8,128)} fusion(bf16[768,1024]{1,0:T(8,128)(2,1)} %all-gather.3.cloned.1.call-done, bf16[1536,768]{1,0:T(8,128)(2,1)S(1)} %copy-done), kind=kOutput, calls=%fused_computation.4 | convolution fusion | flops 2415919104 | bytes 10223616 | tf_op jit(solution)/shard_map/dot_general | solution.py:35
  195.2 47.0 %all-gather.5.cloned.1.call-done = bf16[768,1024]{1,0:T(8,128)(2,1)} async-done(((bf16[768,128]{1,0:T(8,128)(2,1)}), bf16[768,1024]{1,0:T(8,128)(2,1)}) %all-gather.5.cloned.1.call-update) | async-done | bytes 1572880 | tf_op jit(solution)/shard_map/all_gather | solution.py:37
  242.1 6.0 %convolution_bitcast_fusion = f32[1536,1024]{0,1:T(8,128)} fusion(bf16[768,1024]{1,0:T(8,128)(2,1)} %all-gather.5.cloned.1.call-done, bf16[1536,768]{1,0:T(8,128)(2,1)S(1)} %copy-done), kind=kOutput, calls=%fused_computation.3 | convolution fusion | flops 2415919104 | bytes 10223616 | tf_op jit(solution)/shard_map/dot_general | solution.py:35
  248.1 0.0 all-reduce.5.cloned.1.call-update
  248.1 0.0 all-reduce.7.cloned.1.call-start
  248.2 159.2 %all-reduce.5.cloned.1.call-done = (f32[1536,1024]{0,1:T(8,128)}, f32[1536,1024]{0,1:T(8,128)}) async-done(((f32[1536,1024]{0,1:T(8,128)}, f32[1536,1024]{0,1:T(8,128)}), (f32[1536,1024]{0,1:T(8,128)}, f32[1536,1024]{0,1:T(8,128)})) %all-reduce.5.cloned.1.call-update) | async-done | bytes 12582928 | tf_op jit(solution)/shard_map/psum | solution.py:40
  407.4 6.3 %negate_convert_fusion = (bf16[1536,1024]{0,1:T(8,128)(2,1)S(1)}, bf16[1536,1024]{0,1:T(8,128)(2,1)S(1)}) fusion(f32[1536,1024]{0,1:T(8,128)} %get-tuple-element.6, f32[1536,1024]{0,1:T(8,128)} %get-tuple-element.5), kind=kLoop, calls=%fused_computation | loop fusion | flops 6291456 | bytes 18874368 | tf_op jit(solution)/shard_map/convert_element_type | solution.py:41
  413.7 0.0 copy-start.2
  413.7 1.7 dynamic-slice_select_fusion.1
  415.4 0.4 copy-done.2
  415.9 1.5 dynamic-slice_select_fusion
  417.4 0.0 all-reduce.7.cloned.1.call-update
  417.4 151.0 %all-reduce.7.cloned.1.call-done = (bf16[768,1024]{0,1:T(8,128)(2,1)}, bf16[768,1024]{0,1:T(8,128)(2,1)}) async-done(((bf16[768,1024]{0,1:T(8,128)(2,1)}, bf16[768,1024]{0,1:T(8,128)(2,1)}), (bf16[768,1024]{0,1:T(8,128)(2,1)}, bf16[768,1024]{0,1:T(8,128)(2,1)})) %all-reduce.7.cloned.1.call-update) | async-done | bytes 3145744 | tf_op jit(solution)/shard_map/psum | solution.py:19
  568.4 0.0 copy-start.3
  568.4 0.0 copy-start.6
  568.4 4.3 fusion.10
  572.7 0.0 copy-done.3
  572.7 0.0 copy-done.6
  572.7 0.0 copy-start.1
  572.7 6.4 %add_add_fusion = f32[1536,768]{1,0:T(8,128)} fusion(f32[1536,768]{1,0:T(8,128)} %param.7, f32[1536,768]{1,0:T(8,128)S(1)} %fusion.10, bf16[1536,1024]{0,1:T(8,128)(2,1)S(1)} %copy-done.3, bf16[768,1024]{0,1:T(8,128)(2,1)S(1)} %copy-done.6), kind=kOutput, calls=%fused_computation.2 | convolution fusion | flops 2418278400 | bytes 18874368 | tf_op jit(solution)/shard_map/dot_general | solution.py:44
  579.1 0.0 copy-done.1
Async XLA Ops:
  6.5 182.5 %copy-start = (bf16[1536,768]{1,0:T(8,128)(2,1)S(1)}, bf16[1536,768]{1,0:T(8,128)(2,1)}, u32[]{:S(2)}) copy-start(bf16[1536,768]{1,0:T(8,128)(2,1)} %param.4) | copy-start | bytes 7077892
  6.5 3.5 copy-start.4
  6.5 3.5 copy-start.5
  6.5 42.6 %reduce-scatter.5.cloned.1.call-start = ((), (), s32[]{:S(2)}) async-start(), calls=%async_computation.4 | async-start | bytes 3932160 | tf_op jit(solution)/shard_map/reduce_scatter | solution.py:13
  10.0 79.6 %reduce-scatter.9.cloned.1.call-start = ((), (), s32[]{:S(2)}) async-start(), calls=%async_computation.7 | async-start | bytes 3932160 | tf_op jit(solution)/shard_map/reduce_scatter | solution.py:13
  12.3 102.6 %reduce-scatter.7.cloned.1.call-start = ((), (), s32[]{:S(2)}) async-start(), calls=%async_computation.5 | async-start | bytes 1179648 | tf_op jit(solution)/shard_map/reduce_scatter | solution.py:13
  49.2 88.8 %reduce-scatter.11.cloned.1.call-start = ((), (), s32[]{:S(2)}) async-start(), calls=%async_computation.8 | async-start | bytes 1179648 | tf_op jit(solution)/shard_map/reduce_scatter | solution.py:13
  89.6 99.4 %all-gather.3.cloned.1.call-start = ((), (), s32[]{:S(2)}) async-start(), calls=%async_computation.6 | async-start | bytes 1769472 | tf_op jit(solution)/shard_map/all_gather | solution.py:37
  116.6 125.6 %all-gather.5.cloned.1.call-start = ((), (), s32[]{:S(2)}) async-start(), calls=%async_computation.9 | async-start | bytes 1769472 | tf_op jit(solution)/shard_map/all_gather | solution.py:37
  139.7 267.7 %all-reduce.5.cloned.1.call-start = ((), (), s32[]{:S(2)}) async-start(), calls=%async_computation.10 | async-start | bytes 25165824 | tf_op jit(solution)/shard_map/psum | solution.py:40
  248.1 320.3 %all-reduce.7.cloned.1.call-start = ((), (), s32[]{:S(2)}) async-start(), calls=%async_computation.11 | async-start | bytes 6291456 | tf_op jit(solution)/shard_map/psum | solution.py:19
  413.7 2.2 copy-start.2
  568.4 4.3 copy-start.3
  568.4 4.3 copy-start.6
  572.7 6.4 %copy-start.1 = (bf16[1536,768]{1,0:T(8,128)(2,1)S(1)}, bf16[1536,768]{1,0:T(8,128)(2,1)}, u32[]{:S(2)}) copy-start(bf16[1536,768]{1,0:T(8,128)(2,1)} %param.4) | copy-start | bytes 7077892
Sparse Core Ops, SparseCore 0:
  10.1 38.9 reduce-scatter.4
  51.6 37.9 reduce-scatter.8
  91.9 22.8 reduce-scatter.6
  117.0 20.8 reduce-scatter.10
  140.0 48.9 all-gather.2
  191.0 51.0 all-gather.4
  248.2 159.1 all-reduce.4
  417.5 150.8 all-reduce.6
where the time goes:
time: 586 us
  waiting for transfers between devices  530 us (90%)
  matrix products  28.4 us (5%)
  between operations  13.6 us (2%)
  other arithmetic  12.9 us (2%)
    psum x1, waiting for transfers between devices, body(): summed = lax.psum(terms, ('sec', 'col'))  159 us
    psum x1, waiting for transfers between devices, from_root(): return lax.psum(jnp.where(mine, x, jnp.zeros_like(x)), axis)  151 us
    reduce_scatter x4, waiting for transfers between devices, scatter_axes(): x = lax.psum_scatter(x, axis, scatter_dimension=dim, tiled=True)  124 us
    all_gather x2, waiting for transfers between devices, body(): lax.all_gather(scaled, ROW, axis=1, tiled=True)  96.2 us
    dot_general x2, matrix products, body(): jnp.dot(held_inverse, lax.all_gather(scaled, ROW, axis=1, tiled=True), pr...  12.1 us
  transfers between devices with their start and end apart: 8, of which 8 were waited for; matrix products, arithmetic and copies ran while one was open for 2% of the time, Pallas kernels for 0%

commit v1 on v0

--- a/solution.py
+++ b/solution.py
@@ -37,7 +37,7 @@
             lax.all_gather(scaled, ROW, axis=1, tiled=True),
             preferred_element_type=jnp.float32,
         )
-        summed = lax.psum(terms, ("sec", "col"))
+        summed = lax.psum(lax.psum(terms, "col"), "sec")
         inverse = (-summed).astype(jnp.bfloat16)
         own_block = lax.dynamic_slice_in_dim(inverse, offset, tile_cols, 0)
         column_block = from_root(own_block, ROW, root_row)

time: 586 us -> 869 us (1.48)
  waiting for transfers between devices: 530 us -> 814 us
    psum x1 -> x2, waiting for transfers between devices: 159 us -> 442 us  [body(): summed = lax.psum(lax.psum(terms, 'col'), 'sec')]
  transfers between devices with their start and end apart: 8 -> 9, of which waited for: 8 -> 9; matrix products, arithmetic and copies ran while one was open for 2% -> 1% of each run, Pallas kernels for 0% -> 0%
where the time goes in v1:
time: 869 us
  waiting for transfers between devices  814 us (94%)
  matrix products  28.4 us (3%)
  between operations  13.3 us (2%)
  other arithmetic  12.9 us (1%)
    psum x2, waiting for transfers between devices, body(): summed = lax.psum(lax.psum(terms, 'col'), 'sec')  442 us
    psum x1, waiting for transfers between devices, from_root(): return lax.psum(jnp.where(mine, x, jnp.zeros_like(x)), axis)  151 us
    reduce_scatter x4, waiting for transfers between devices, scatter_axes(): x = lax.psum_scatter(x, axis, scatter_dimension=dim, tiled=True)  124 us
    all_gather x2, waiting for transfers between devices, body(): lax.all_gather(scaled, ROW, axis=1, tiled=True)  96.3 us
  transfers between devices with their start and end apart: 9, of which 9 were waited for; matrix products, arithmetic and copies ran while one was open for 1% of the time, Pallas kernels for 0%

profile of v1, /device:TPU:5, one launch (start us, length us, event | category | flops | bytes accessed | tf_op | source)
XLA Modules:
  0.0 869.1 jit_solution(11526498549195027710)
XLA Ops:
  6.5 0.0 copy-start
  6.5 0.0 copy-start.4
  6.5 0.0 copy-start.5
  6.5 0.0 reduce-scatter.5.cloned.1.call-start
  6.5 3.4 fusion.2
  10.0 0.0 reduce-scatter.5.cloned.1.call-update
  10.0 0.0 reduce-scatter.9.cloned.1.call-start
  10.0 0.0 copy-done.4
  10.0 0.0 copy-done.5
  10.1 2.2 fusion
  12.3 0.0 reduce-scatter.9.cloned.1.call-update
  12.3 0.0 reduce-scatter.7.cloned.1.call-start
  12.3 36.8 %reduce-scatter.5.cloned.1.call-done = f32[768,256]{1,0:T(8,128)} async-done(((f32[768,1024]{1,0:T(8,128)}), f32[768,256]{1,0:T(8,128)}) %reduce-scatter.5.cloned.1.call-update) | async-done | bytes 786448 | tf_op jit(solution)/shard_map/reduce_scatter | solution.py:13
  49.2 0.0 reduce-scatter.7.cloned.1.call-update
  49.2 0.0 reduce-scatter.11.cloned.1.call-start
  49.2 40.3 %reduce-scatter.9.cloned.1.call-done = f32[768,256]{1,0:T(8,128)} async-done(((f32[768,1024]{1,0:T(8,128)}), f32[768,256]{1,0:T(8,128)}) %reduce-scatter.9.cloned.1.call-update) | async-done | bytes 786448 | tf_op jit(solution)/shard_map/reduce_scatter | solution.py:13
  89.6 0.0 reduce-scatter.11.cloned.1.call-update
  89.6 0.0 all-gather.3.cloned.1.call-start
  89.6 25.2 %reduce-scatter.7.cloned.1.call-done = f32[768,128]{1,0:T(8,128)} async-done(((f32[768,256]{1,0:T(8,128)}), f32[768,128]{1,0:T(8,128)}) %reduce-scatter.7.cloned.1.call-update) | async-done | bytes 393232 | tf_op jit(solution)/shard_map/reduce_scatter | solution.py:13
  114.8 1.7 convert_element_type.12
  116.5 0.0 all-gather.3.cloned.1.call-update
  116.6 0.0 all-gather.5.cloned.1.call-start
  116.6 21.3 %reduce-scatter.11.cloned.1.call-done = f32[768,128]{1,0:T(8,128)} async-done(((f32[768,256]{1,0:T(8,128)}), f32[768,128]{1,0:T(8,128)}) %reduce-scatter.11.cloned.1.call-update) | async-done | bytes 393232 | tf_op jit(solution)/shard_map/reduce_scatter | solution.py:13
  138.0 1.7 convert_element_type.14
  139.7 0.0 all-gather.5.cloned.1.call-update
  139.7 0.0 all-reduce.7.cloned.1.call-start
  139.7 49.3 %all-gather.3.cloned.1.call-done = bf16[768,1024]{1,0:T(8,128)(2,1)} async-done(((bf16[768,128]{1,0:T(8,128)(2,1)}), bf16[768,1024]{1,0:T(8,128)(2,1)}) %all-gather.3.cloned.1.call-update) | async-done | bytes 1572880 | tf_op jit(solution)/shard_map/all_gather | solution.py:37
  189.0 0.0 copy-done
  189.0 6.0 convolution_bitcast_fusion.1
  195.0 47.1 %all-gather.5.cloned.1.call-done = bf16[768,1024]{1,0:T(8,128)(2,1)} async-done(((bf16[768,128]{1,0:T(8,128)(2,1)}), bf16[768,1024]{1,0:T(8,128)(2,1)}) %all-gather.5.cloned.1.call-update) | async-done | bytes 1572880 | tf_op jit(solution)/shard_map/all_gather | solution.py:37
  242.1 6.1 convolution_bitcast_fusion
  248.2 0.0 all-reduce.7.cloned.1.call-update
  248.2 0.0 all-reduce.9.cloned.1.call-start
  248.3 144.9 %all-reduce.7.cloned.1.call-done = (f32[1536,1024]{0,1:T(8,128)}, f32[1536,1024]{0,1:T(8,128)}) async-done(((f32[1536,1024]{0,1:T(8,128)}, f32[1536,1024]{0,1:T(8,128)}), (f32[1536,1024]{0,1:T(8,128)}, f32[1536,1024]{0,1:T(8,128)})) %all-reduce.7.cloned.1.call-update) | async-done | bytes 12582928 | tf_op jit(solution)/shard_map/psum | solution.py:40
  393.2 0.0 all-reduce.9.cloned.1.call-update
  393.2 0.0 all-reduce.11.cloned.1.call-start
  393.3 297.4 %all-reduce.9.cloned.1.call-done = (f32[1536,1024]{0,1:T(8,128)}, f32[1536,1024]{0,1:T(8,128)}) async-done(((f32[1536,1024]{0,1:T(8,128)}, f32[1536,1024]{0,1:T(8,128)}), (f32[1536,1024]{0,1:T(8,128)}, f32[1536,1024]{0,1:T(8,128)})) %all-reduce.9.cloned.1.call-update) | async-done | bytes 12582928 | tf_op jit(solution)/shard_map/psum | solution.py:40
  690.7 6.3 negate_convert_fusion
  697.0 0.0 copy-start.2
  697.0 1.7 dynamic-slice_select_fusion.1
  698.7 0.4 copy-done.2
  699.2 1.5 dynamic-slice_select_fusion
  700.7 0.0 all-reduce.11.cloned.1.call-update
  700.7 151.2 %all-reduce.11.cloned.1.call-done = (bf16[768,1024]{0,1:T(8,128)(2,1)}, bf16[768,1024]{0,1:T(8,128)(2,1)}) async-done(((bf16[768,1024]{0,1:T(8,128)(2,1)}, bf16[768,1024]{0,1:T(8,128)(2,1)}), (bf16[768,1024]{0,1:T(8,128)(2,1)}, bf16[768,1024]{0,1:T(8,128)(2,1)})) %all-reduce.11.cloned.1.call-update) | async-done | bytes 3145744 | tf_op jit(solution)/shard_map/psum | solution.py:19
  851.9 0.0 copy-start.3
  851.9 0.0 copy-start.6
  851.9 4.3 fusion.10
  856.2 0.0 copy-done.3
  856.2 0.0 copy-done.6
  856.2 0.0 copy-start.1
  856.2 6.4 add_add_fusion
  862.6 0.0 copy-done.1
Async XLA Ops:
  6.5 182.5 %copy-start = (bf16[1536,768]{1,0:T(8,128)(2,1)S(1)}, bf16[1536,768]{1,0:T(8,128)(2,1)}, u32[]{:S(2)}) copy-start(bf16[1536,768]{1,0:T(8,128)(2,1)} %param.4) | copy-start | bytes 7077892
  6.5 3.5 copy-start.4
  6.5 3.5 copy-start.5
  6.5 42.6 %reduce-scatter.5.cloned.1.call-start = ((), (), s32[]{:S(2)}) async-start(), calls=%async_computation.4 | async-start | bytes 3932160 | tf_op jit(solution)/shard_map/reduce_scatter | solution.py:13
  10.0 79.6 %reduce-scatter.9.cloned.1.call-start = ((), (), s32[]{:S(2)}) async-start(), calls=%async_computation.7 | async-start | bytes 3932160 | tf_op jit(solution)/shard_map/reduce_scatter | solution.py:13
  12.3 102.6 %reduce-scatter.7.cloned.1.call-start = ((), (), s32[]{:S(2)}) async-start(), calls=%async_computation.5 | async-start | bytes 1179648 | tf_op jit(solution)/shard_map/reduce_scatter | solution.py:13
  49.2 88.8 %reduce-scatter.11.cloned.1.call-start = ((), (), s32[]{:S(2)}) async-start(), calls=%async_computation.8 | async-start | bytes 1179648 | tf_op jit(solution)/shard_map/reduce_scatter | solution.py:13
  89.6 99.4 %all-gather.3.cloned.1.call-start = ((), (), s32[]{:S(2)}) async-start(), calls=%async_computation.6 | async-start | bytes 1769472 | tf_op jit(solution)/shard_map/all_gather | solution.py:37
  116.6 125.6 %all-gather.5.cloned.1.call-start = ((), (), s32[]{:S(2)}) async-start(), calls=%async_computation.9 | async-start | bytes 1769472 | tf_op jit(solution)/shard_map/all_gather | solution.py:37
  139.7 253.5 %all-reduce.7.cloned.1.call-start = ((), (), s32[]{:S(2)}) async-start(), calls=%async_computation.10 | async-start | bytes 25165824 | tf_op jit(solution)/shard_map/psum | solution.py:40
  248.2 442.5 %all-reduce.9.cloned.1.call-start = ((), (), s32[]{:S(2)}) async-start(), calls=%async_computation.11 | async-start | bytes 25165824 | tf_op jit(solution)/shard_map/psum | solution.py:40
  393.2 458.7 %all-reduce.11.cloned.1.call-start = ((), (), s32[]{:S(2)}) async-start(), calls=%async_computation.12 | async-start | bytes 6291456 | tf_op jit(solution)/shard_map/psum | solution.py:19
  697.0 2.2 copy-start.2
  851.9 4.3 copy-start.3
  851.9 4.4 copy-start.6
  856.2 6.4 copy-start.1
Sparse Core Ops, SparseCore 0:
  10.1 38.9 reduce-scatter.4
  51.6 37.9 reduce-scatter.8
  91.9 22.8 reduce-scatter.6
  117.0 20.8 reduce-scatter.10
  140.0 48.9 all-gather.2
  191.0 51.0 all-gather.4
  248.3 144.8 all-reduce.6
  395.8 294.8 all-reduce.8
  700.8 151.0 all-reduce.10
